TPU v7x, 32 devices: a whole 2x2x4 slice. The times are simulated.
32 devices in a mesh: dp: 16 (over z, x, core), shard: 2 (over y).
Axes of the slice: x: 2, y: 2, z: 4, core: 2. Of those that a mesh axis runs over, the one named last changes fastest.
Arguments:
- tokens: bfloat16 [4096, 1088], P(('dp', 'shard')), may hold values from -6 to 6
- seq_ends: int32 [32, 3], P(('dp', 'shard')), may hold values from 0 to 128, as said below
- attn_weight: bfloat16 [1, 4352, 1088], P(None, ('dp', 'shard'))
- up_weight: bfloat16 [1, 4352, 1088], P(None, ('dp', 'shard')), may hold values from -0.1875 to 0.1875
- down_weight: bfloat16 [1, 4352, 1088], P(None, ('dp', 'shard')), may hold values from -0.09375 to 0.09375
- vectors: bfloat16 [1, 13056], P(None, ('dp', 'shard'))
- cotangent: bfloat16 [4096, 1088], P(('dp', 'shard')), may hold values from -6 to 6
Outputs:
- output: bfloat16 [4096, 1088], P(('dp', 'shard'))
- grad_tokens: float32 [4096, 1088], P(('dp', 'shard'))
- grad_attn: float32 [1, 4352, 1088], P(None, ('dp', 'shard'))
- grad_up: float32 [1, 4352, 1088], P(None, ('dp', 'shard'))
- grad_down: float32 [1, 4352, 1088], P(None, ('dp', 'shard'))
- grad_vectors: float32 [1, 13056], P(None, ('dp', 'shard'))
Inputs may be any that keep to these rules, and one draw needn't show every extreme that they name: `seq_ends`: each row lists non-decreasing end offsets of the sequences packed into one device's 128 slots; slots from the row's last end onward form one more segment.
All inputs are finite; a program needn't handle non-finite values.
Results may differ from a plain program's by a relative error of at most 0.0089.
Values may be sent and summed in bfloat16 or wider, within the bound.
A program may use at most 192 MiB of HBM per device.

v0:
```python
import jax
import jax.numpy as jnp
from jax import lax
from jax.sharding import PartitionSpec as P

HEAD_DIM = 64
EPS = 1e-05


def layer_norm(values, gain, shift):
    average = jnp.mean(values, axis=-1, keepdims=True)
    centred = values - average
    variance = jnp.mean(centred * centred, axis=-1, keepdims=True)
    return centred * lax.rsqrt(variance + EPS) * gain + shift


def gelu_tanh(values):
    return (
        0.5
        * values
        * (1.0 + jnp.tanh(0.7978845608028654 * (values + 0.044715 * values * values * values)))
    )


def contract_last(left, right):
    return lax.dot_general(
        left, right, (((1,), (1,)), ((), ())), preferred_element_type=jnp.float32
    )


def contract_first(left, right):
    return lax.dot_general(
        left, right, (((0,), (0,)), ((), ())), preferred_element_type=jnp.float32
    )


def head_product(form, left, right):
    return jnp.einsum(form, left, right, preferred_element_type=jnp.float32)


def causal_mask(ends_row, slot_count):
    positions = jnp.arange(slot_count, dtype=jnp.int32)
    segment = jnp.sum((ends_row[None, :] <= positions[:, None]).astype(jnp.int32), axis=1)
    return (segment[:, None] == segment[None, :]) & (positions[None, :] <= positions[:, None])


def split_vectors(vectors, model_width):
    vector_f32 = vectors.astype(jnp.float32)
    parts_list = [
        vector_f32[slot_idx * model_width : (slot_idx + 1) * model_width] for slot_idx in range(8)
    ]
    return parts_list + [vector_f32[8 * model_width :]]


def forward_layer(hidden, params, allowed):
    attn_part, up_part, down_part, vector_part = params
    model_width = attn_part.shape[1]
    head_count = model_width // HEAD_DIM
    row_count = hidden.shape[0]
    (
        gain_one,
        shift_one,
        query_bias,
        value_bias,
        out_bias,
        gain_two,
        shift_two,
        down_bias,
        up_bias,
    ) = split_vectors(vector_part, model_width)
    normed_one = layer_norm(hidden, gain_one, shift_one).astype(jnp.bfloat16)
    projected = contract_last(normed_one, attn_part[: 3 * model_width])
    query_heads = (
        ((projected[:, :model_width] + query_bias) * HEAD_DIM ** (-0.5))
        .astype(jnp.bfloat16)
        .reshape(row_count, head_count, HEAD_DIM)
    )
    key_heads = (
        projected[:, model_width : 2 * model_width]
        .astype(jnp.bfloat16)
        .reshape(row_count, head_count, HEAD_DIM)
    )
    value_heads = (
        (projected[:, 2 * model_width :] + value_bias)
        .astype(jnp.bfloat16)
        .reshape(row_count, head_count, HEAD_DIM)
    )
    scores = jnp.where(allowed[None], head_product("qhc,khc->hqk", query_heads, key_heads), -1e30)
    log_total = jnp.log(jnp.sum(jnp.exp(scores), axis=-1))
    weights = jnp.exp(scores - log_total[..., None]).astype(jnp.bfloat16)
    context = (
        head_product("hqk,khc->qhc", weights, value_heads)
        .reshape(row_count, model_width)
        .astype(jnp.bfloat16)
    )
    after_attn = (
        hidden
        + jnp.dot(context, attn_part[3 * model_width :], preferred_element_type=jnp.float32)
        + out_bias
    )
    normed_two = layer_norm(after_attn, gain_two, shift_two).astype(jnp.bfloat16)
    pre_act = contract_last(normed_two, up_part) + up_bias
    activated = gelu_tanh(pre_act).astype(jnp.bfloat16)
    result = (
        after_attn + jnp.dot(activated, down_part, preferred_element_type=jnp.float32) + down_bias
    )
    saved_acts = (
        hidden,
        normed_one,
        query_heads,
        key_heads,
        value_heads,
        log_total,
        context,
        after_attn,
        normed_two,
        pre_act,
        activated,
    )
    return (result, saved_acts)


def backward_layer(upstream, params, saved_acts, allowed):
    attn_part, up_part, down_part, vector_part = params
    (
        hidden,
        normed_one,
        query_heads,
        key_heads,
        value_heads,
        log_total,
        context,
        after_attn,
        normed_two,
        pre_act,
        activated,
    ) = saved_acts
    model_width = attn_part.shape[1]
    head_count = model_width // HEAD_DIM
    row_count = hidden.shape[0]
    (
        gain_one,
        shift_one,
        query_bias,
        value_bias,
        out_bias,
        gain_two,
        shift_two,
        down_bias,
        up_bias,
    ) = split_vectors(vector_part, model_width)
    upstream_bf = upstream.astype(jnp.bfloat16)
    grad_down_bias = jnp.sum(upstream, axis=0)
    grad_act = contract_last(upstream_bf, down_part)
    grad_pre = jax.vjp(gelu_tanh, pre_act)[1](grad_act)[0]
    grad_up_bias = jnp.sum(grad_pre, axis=0)
    grad_pre_bf = grad_pre.astype(jnp.bfloat16)
    grad_normed_two = jnp.dot(grad_pre_bf, up_part, preferred_element_type=jnp.float32)
    back_two = jax.vjp(layer_norm, after_attn, gain_two, shift_two)[1]
    grad_mid, grad_gain_two, grad_shift_two = back_two(grad_normed_two)
    grad_mid = upstream + grad_mid
    grad_out_bias = jnp.sum(grad_mid, axis=0)
    grad_mid_bf = grad_mid.astype(jnp.bfloat16)
    grad_context = (
        contract_last(grad_mid_bf, attn_part[3 * model_width :])
        .astype(jnp.bfloat16)
        .reshape(row_count, head_count, HEAD_DIM)
    )
    scores = jnp.where(allowed[None], head_product("qhc,khc->hqk", query_heads, key_heads), -1e30)
    probs_f32 = jnp.exp(scores - log_total[..., None])
    probs_bf = probs_f32.astype(jnp.bfloat16)
    grad_values = head_product("hqk,qhc->khc", probs_bf, grad_context).reshape(
        row_count, model_width
    )
    grad_probs = head_product("qhc,khc->hqk", grad_context, value_heads)
    row_dot = jnp.sum(probs_f32 * grad_probs, axis=-1, keepdims=True)
    grad_scores = (probs_f32 * (grad_probs - row_dot)).astype(jnp.bfloat16)
    grad_query = head_product("hqk,khc->qhc", grad_scores, key_heads).reshape(
        row_count, model_width
    ) * HEAD_DIM ** (-0.5)
    grad_keys = head_product("hqk,qhc->khc", grad_scores, query_heads).reshape(
        row_count, model_width
    )
    grad_query_bias = jnp.sum(grad_query, axis=0)
    grad_value_bias = jnp.sum(grad_values, axis=0)
    grad_proj = jnp.concatenate([grad_query, grad_keys, grad_values], axis=1).astype(jnp.bfloat16)
    grad_normed_one = jnp.dot(
        grad_proj, attn_part[: 3 * model_width], preferred_element_type=jnp.float32
    )
    back_one = jax.vjp(layer_norm, hidden, gain_one, shift_one)[1]
    grad_below, grad_gain_one, grad_shift_one = back_one(grad_normed_one)
    grad_below = grad_mid + grad_below
    left_all = jnp.concatenate([grad_proj, context], axis=1)
    grad_vector = jnp.concatenate(
        [
            grad_gain_one,
            grad_shift_one,
            grad_query_bias,
            grad_value_bias,
            grad_out_bias,
            grad_gain_two,
            grad_shift_two,
            grad_down_bias,
            grad_up_bias,
        ]
    )
    operands = (left_all, normed_one, grad_mid_bf, grad_pre_bf, normed_two, activated, upstream_bf)
    return (grad_below, operands, grad_vector)


def shards(tokens, seq_ends, attn_weight, up_weight, down_weight, vectors, cotangent):
    allowed = causal_mask(seq_ends[0], tokens.shape[0])
    model_width = tokens.shape[1]
    attn_rows = attn_weight.shape[1]
    layer_count = attn_weight.shape[0]
    hidden = tokens.astype(jnp.float32)
    kept_params = []
    layer_idx = 0
    gathered = (
        lax.all_gather(attn_weight[layer_idx], ("dp", "shard"), axis=0, tiled=True),
        lax.all_gather(up_weight[layer_idx], ("dp", "shard"), axis=0, tiled=True),
        lax.all_gather(down_weight[layer_idx], ("dp", "shard"), axis=0, tiled=True),
        lax.all_gather(vectors[layer_idx], ("dp", "shard"), axis=0, tiled=True),
    )
    kept_params.append(gathered)
    hidden, saved_acts = forward_layer(hidden, gathered, allowed)
    saved_list = [saved_acts]
    output = hidden.astype(jnp.bfloat16)
    upstream = cotangent.astype(jnp.float32)
    grad_sets = [None] * layer_count
    for layer_idx in reversed(range(layer_count)):
        gathered = (
            lax.all_gather(attn_weight[layer_idx], ("dp", "shard"), axis=0, tiled=True),
            lax.all_gather(up_weight[layer_idx], ("dp", "shard"), axis=0, tiled=True),
            lax.all_gather(down_weight[layer_idx], ("dp", "shard"), axis=0, tiled=True),
            lax.all_gather(vectors[layer_idx], ("dp", "shard"), axis=0, tiled=True),
        )
        upstream, operands, grad_vector = backward_layer(
            upstream, gathered, saved_list[layer_idx], allowed
        )
        left_all, normed_one, grad_mid_bf, grad_pre_bf, normed_two, activated, upstream_bf = (
            operands
        )
        row_index = jnp.arange(attn_rows * lax.axis_size(("dp", "shard")), dtype=jnp.int32)
        first_rows = jnp.where(
            (row_index < 3 * model_width)[None, :], left_all, jnp.zeros_like(left_all)
        )
        second_rows = jnp.where(
            (row_index >= 3 * model_width)[None, :], left_all, jnp.zeros_like(left_all)
        )
        grad_attn_w = lax.psum_scatter(
            contract_first(first_rows, normed_one) + contract_first(second_rows, grad_mid_bf),
            ("dp", "shard"),
            scatter_dimension=0,
            tiled=True,
        )
        grad_up_w = lax.psum_scatter(
            contract_first(grad_pre_bf, normed_two),
            ("dp", "shard"),
            scatter_dimension=0,
            tiled=True,
        )
        grad_down_w = lax.psum_scatter(
            contract_first(activated, upstream_bf), ("dp", "shard"), scatter_dimension=0, tiled=True
        )
        grad_vec_own = lax.psum_scatter(
            grad_vector, ("dp", "shard"), scatter_dimension=0, tiled=True
        )
        grad_sets[layer_idx] = (grad_attn_w, grad_up_w, grad_down_w, grad_vec_own)
    grad_attn = jnp.stack([grad_sets[0][0]])
    grad_up = jnp.stack([grad_sets[0][1]])
    grad_down = jnp.stack([grad_sets[0][2]])
    grad_vectors = jnp.stack([grad_sets[0][3]])
    return (output, upstream, grad_attn, grad_up, grad_down, grad_vectors)


def solution(mesh):
    return jax.shard_map(
        shards,
        mesh=mesh,
        in_specs=(
            P(("dp", "shard"), None),
            P(("dp", "shard"), None),
            P(None, ("dp", "shard"), None),
            P(None, ("dp", "shard"), None),
            P(None, ("dp", "shard"), None),
            P(None, ("dp", "shard")),
            P(("dp", "shard"), None),
        ),
        out_specs=(
            P(("dp", "shard"), None),
            P(("dp", "shard"), None),
            P(None, ("dp", "shard"), None),
            P(None, ("dp", "shard"), None),
            P(None, ("dp", "shard"), None),
            P(None, ("dp", "shard")),
        ),
        check_vma=False,
    )
```

profile of v0, /device:TPU:0, one launch (start us, length us, event | category | flops | bytes accessed | tf_op | source)
XLA Modules:
  0.0 987.9 jit_solution(13790586589980789792)
XLA Ops:
  10.4 43.7 %all-reduce = bf16[13056]{0:T(1024)(128)(2,1)S(1)} all-reduce(bf16[13056]{0:T(1024)(128)(2,1)S(1)} %dynamic-update-slice), channel_id=2, replica_groups=mesh['dp'=16,'shard'=2] {'dp','shard'}, use_global_device_ids=true, to_apply=%add | all-reduce | flops 13056 | bytes 52224
  57.4 40.9 %all-gather.8.cloned.1.call-done = bf16[1,4352,1088]{2,1,0:T(8,128)(2,1)} async-done(((bf16[1,136,1088]{2,1,0:T(8,128)(2,1)}), bf16[1,4352,1088]{2,1,0:T(8,128)(2,1)}) %all-gather.8.cloned.1.call-update) | async-done | bytes 9469968 | tf_op jit(solution)/shard_map/all_gather | solution.py:220
  98.4 5.4 fusion.10
  105.2 3.0 fusion.94
  108.3 75.5 %all-gather.10.cloned.1.call-done = bf16[1,4352,1088]{2,1,0:T(8,128)(2,1)} async-done(((bf16[1,136,1088]{2,1,0:T(8,128)(2,1)}), bf16[1,4352,1088]{2,1,0:T(8,128)(2,1)}) %all-gather.10.cloned.1.call-update) | async-done | bytes 9469968 | tf_op jit(solution)/shard_map/all_gather | solution.py:221
  183.9 7.2 fusion.11
  191.1 78.3 %all-gather.12.cloned.1.call-done = bf16[1,4352,1088]{2,1,0:T(8,128)(2,1)} async-done(((bf16[1,136,1088]{2,1,0:T(8,128)(2,1)}), bf16[1,4352,1088]{2,1,0:T(8,128)(2,1)}) %all-gather.12.cloned.1.call-update) | async-done | bytes 9469968 | tf_op jit(solution)/shard_map/all_gather | solution.py:222
  269.4 7.4 fusion.97
  276.8 4.7 multiply_reduce_fusion.1
  282.8 3.3 convolution_convert_fusion
  286.1 3.0 fusion.92
  289.1 1.4 fusion.98
  290.5 1.3 multiply_reduce_fusion
  293.7 14.5 %fusion.35 = f32[4352,1088]{1,0:T(8,128)} fusion(pred[4352]{0:T(1024)(128)(4,1)S(1)} %iota_compare_fusion.2, bf16[128,1088]{0,1:T(8,128)(2,1)S(1)} %bitcast.88, bf16[128,1088]{0,1:T(8,128)(2,1)S(1)} %bitcast.85, bf16[128,1088]{0,1:T(8,128)(2,1)S(1)} %bitcast.74, bf16[128,1088]{0,1:T(8,128)(2,1)S(1)} %bitcast.77, bf16[128,1088]{0,1:T(8,128)(2,1)S(1)} %copy-done.1, ...), kind=kOutput, calls=%fused_computation.41 | convolution fusion | flops 1218002944 | bytes 20346624 | tf_op jit(solution)/shard_map/dot_general | solution.py:32
  308.2 20.0 %convolution_add_fusion = f32[4352,1088]{1,0:T(8,128)} fusion(f32[4352,1088]{1,0:T(8,128)} %fusion.35, bf16[128,1088]{0,1:T(8,128)(2,1)S(1)} %copy-done.18, pred[4352]{0:T(1024)(128)(4,1)S(1)} %iota_compare_fusion.1, bf16[128,1088]{0,1:T(8,128)(2,1)S(1)} %bitcast.89, bf16[128,1088]{0,1:T(8,128)(2,1)S(1)} %bitcast.86, bf16[128,1088]{0,1:T(8,128)(2,1)S(1)} %bitcast.75, ...), kind=kOutput, calls=%fused_computation.1 | convolution fusion | flops 1221902336 | bytes 39276800 | tf_op jit(solution)/shard_map/dot_general | solution.py:32
  328.2 12.6 %fusion.61 = f32[4352,1088]{1,0:T(8,128)} fusion(bf16[128,4352]{1,0:T(8,128)(2,1)} %copy-done.4, f32[128,1088]{0,1:T(8,128)S(1)} %get-tuple-element.33, f32[1088]{0:T(1024)S(1)} %get-tuple-element.16, f32[1088]{0:T(1024)S(1)} %get-tuple-element.15, f32[128]{0:T(128)S(1)} %fusion.81, f32[128]{0:T(128)S(1)} %broadcast_multiply_fusion), kind=kOutput, calls=%fused_computation.82 | convolution fusion | flops 1212850176 | bytes 20620800 | tf_op jit(solution)/shard_map/dot_general | solution.py:32
  340.9 11.0 %fusion.89 = f32[4352,1088]{1,0:T(8,128)} fusion(bf16[128,1088]{0,1:T(8,128)(2,1)} %param.13, f32[128,4352]{1,0:T(8,128)S(1)} %fusion.11), kind=kOutput, calls=%fused_computation.124 | convolution fusion | flops 1217167360 | bytes 21446656 | tf_op jit(solution)/shard_map/dot_general | solution.py:32
  352.1 7.2 fusion.90
  359.8 1.2 convert_reduce_fusion.1
  361.1 40.9 %all-reduce.4 = f32[13056]{0:T(1024)S(1)} all-reduce(f32[13056]{0:T(1024)S(1)} %concatenate.13), channel_id=9, replica_groups=mesh['dp'=16,'shard'=2] {'dp','shard'}, use_global_device_ids=true, to_apply=%region_23.24.clone | all-reduce | flops 13056 | bytes 104448
  402.6 8.3 fusion.21
  411.0 130.0 %reduce-scatter.10.cloned.1.call-done = f32[136,1088]{1,0:T(8,128)} async-done(((f32[4352,1088]{1,0:T(8,128)}), f32[136,1088]{1,0:T(8,128)}) %reduce-scatter.10.cloned.1.call-update) | async-done | bytes 591888
  540.9 219.9 %reduce-scatter.12.cloned.1.call-done = f32[136,1088]{1,0:T(8,128)} async-done(((f32[4352,1088]{1,0:T(8,128)}), f32[136,1088]{1,0:T(8,128)}) %reduce-scatter.12.cloned.1.call-update) | async-done | bytes 591888
  760.9 219.9 %reduce-scatter.14.cloned.1.call-done = f32[136,1088]{1,0:T(8,128)} async-done(((f32[4352,1088]{1,0:T(8,128)}), f32[136,1088]{1,0:T(8,128)}) %reduce-scatter.14.cloned.1.call-update) | async-done | bytes 591888
  (89 shorter events, 12.3 us)
Async XLA Ops:
  7.2 91.2 %all-gather.8.cloned.1.call-start = ((), (), s32[]{:S(2)}) async-start(), calls=%async_computation.3 | async-start | bytes 10340352 | tf_op jit(solution)/shard_map/all_gather | solution.py:220
  7.9 176.0 %all-gather.10.cloned.1.call-start = ((), (), s32[]{:S(2)}) async-start(), calls=%async_computation.4 | async-start | bytes 10340352 | tf_op jit(solution)/shard_map/all_gather | solution.py:221
  8.6 260.7 %all-gather.12.cloned.1.call-start = ((), (), s32[]{:S(2)}) async-start(), calls=%async_computation.5 | async-start | bytes 10340352 | tf_op jit(solution)/shard_map/all_gather | solution.py:222
  9.4 531.5 %reduce-scatter.10.cloned.1.call-start = ((), (), s32[]{:S(2)}) async-start(), calls=%async_computation.6 | async-start | bytes 20680704
  103.9 1.3 copy-start.10
  103.9 1.3 copy-start.1
  104.3 3.9 copy-start.19
  104.6 3.5 copy-start.5
  105.1 3.2 copy-start.15
  183.9 85.5 %copy-start.12 = (bf16[128,1088]{0,1:T(8,128)(2,1)S(1)}, bf16[128,1088]{0,1:T(8,128)(2,1)}, u32[]{:S(2)}) copy-start(bf16[128,1088]{0,1:T(8,128)(2,1)} %param.13) | copy-start | bytes 835588
  269.4 7.5 copy-start
  276.8 4.8 copy-start.4
  282.7 3.4 copy-start.17
  282.7 6.4 copy-start.20
  289.1 1.4 copy-start.6
  291.9 1.4 copy-start.11
  291.9 1.8 copy-start.14
  291.9 1.8 copy-start.16
  293.7 14.5 %copy-start.7 = (bf16[17,64,128]{2,1,0:T(8,128)(2,1)}, bf16[17,64,128]{2,1,0:T(8,128)(2,1)S(1)}, u32[]{:S(2)}) copy-start(bf16[17,64,128]{2,1,0:T(8,128)(2,1)S(1)} %get-tuple-element.31) | copy-start | bytes 835588
  293.7 14.5 %copy-start.18 = (bf16[128,1088]{0,1:T(8,128)(2,1)S(1)}, bf16[128,1088]{0,1:T(8,128)(2,1)}, u32[]{:S(2)}) copy-start(bf16[128,1088]{0,1:T(8,128)(2,1)} %copy-done.17) | copy-start | bytes 835588
  328.2 432.7 %reduce-scatter.12.cloned.1.call-start = ((), (), s32[]{:S(2)}) async-start(), calls=%async_computation.7 | async-start | bytes 20680704
  340.8 639.9 %reduce-scatter.14.cloned.1.call-start = ((), (), s32[]{:S(2)}) async-start(), calls=%async_computation.8 | async-start | bytes 20680704
  352.1 7.7 copy-start.3
  352.1 7.7 copy-start.13
  (3 other events, 2.7 us)
Sparse Core Ops, SparseCore 0:
  10.8 87.5 all-gather.7
  101.2 82.5 all-gather.9
  186.7 82.5 all-gather.11
  328.3 212.5 reduce-scatter.9
  547.8 213.0 reduce-scatter.11
  767.7 213.0 reduce-scatter.13
where the time goes:
time: 998 us; the launch traced here: 988 us
  waiting for transfers between devices  767 us (77%)
  matrix products  111 us (11%)
  blocking collectives  84.6 us (8%)
  between operations  14.8 us (1%)
    unnamed x9, waiting for transfers between devices  572 us
    unnamed x2, blocking collectives  84.6 us
    all_gather x1, waiting for transfers between devices, shards(): lax.all_gather(down_weight[layer_idx], ('dp', 'shard'), axis=0, tiled=True)  78.3 us
    all_gather x1, waiting for transfers between devices, shards(): lax.all_gather(up_weight[layer_idx], ('dp', 'shard'), axis=0, tiled=True)  75.5 us
    dot_general x4, matrix products, contract_first(): lax.dot_general(left, right, (((0,), (0,)), ((), ())), preferred_element_...  58 us
    all_gather x1, waiting for transfers between devices, shards(): lax.all_gather(attn_weight[layer_idx], ('dp', 'shard'), axis=0, tiled=True)  40.9 us
    dot_general x4, matrix products, contract_last(): lax.dot_general(left, right, (((1,), (1,)), ((), ())), preferred_element_...  23.5 us
  transfers between devices with their start and end apart: 6, of which 6 were waited for; matrix products, arithmetic and copies ran while one was open for 6% of the time, Pallas kernels for 0%

commit v1 on v0

--- a/solution.py
+++ b/solution.py
@@ -5,6 +5,28 @@
 
 HEAD_DIM = 64
 EPS = 1e-05
+
+
+def laid_out(pieces, dim):
+    dims = list(pieces.shape[1:])
+    dims[dim] *= pieces.shape[0]
+    return jnp.moveaxis(pieces, 0, dim).reshape(dims)
+
+
+def grow_blocks(array, axis):
+    size = lax.axis_size(axis)
+    parts = array[None]
+    for level in range(size.bit_length() - 1):
+        apart = 1 << level
+        other = lax.ppermute(parts, axis, [(i, i ^ apart) for i in range(size)])
+        both = jnp.stack([parts, other])
+        upper = lax.axis_index(axis) >> level & 1
+        parts = jnp.where(upper == 0, both, both[::-1]).reshape(-1, *array.shape)
+    return parts
+
+
+def doubled_up(shard, axis, dim):
+    return laid_out(grow_blocks(shard, axis), dim)
 
 
 def layer_norm(values, gain, shift):
@@ -219,7 +241,7 @@
     gathered = (
         lax.all_gather(attn_weight[layer_idx], ("dp", "shard"), axis=0, tiled=True),
         lax.all_gather(up_weight[layer_idx], ("dp", "shard"), axis=0, tiled=True),
-        lax.all_gather(down_weight[layer_idx], ("dp", "shard"), axis=0, tiled=True),
+        doubled_up(down_weight[layer_idx], ("dp", "shard"), 0),
         lax.all_gather(vectors[layer_idx], ("dp", "shard"), axis=0, tiled=True),
     )
     kept_params.append(gathered)

time: 998 us -> 1220 us (1.22)
  waiting for transfers between devices: 767 us -> 954 us
  other arithmetic: 7.82 us -> 37.5 us
    ppermute x0 -> x5, waiting for transfers between devices: none -> 396 us  [grow_blocks(): other = lax.ppermute(parts, axis, [(i, i ^ apart) for i in range(size)])]
    unnamed x9, waiting for transfers between devices: 572 us -> 364 us
    select_n x0 -> x4, other arithmetic: none -> 17.9 us  [grow_blocks(): parts = jnp.where(upper == 0, both, both[::-1]).reshape(-1, *array.shape)]
  transfers between devices with their start and end apart: 6 -> 11, of which waited for: 6 -> 10; matrix products, arithmetic and copies ran while one was open for 6% -> 8% of each run, Pallas kernels for 0% -> 0%
where the time goes in v1:
time: 1220 us; the launch traced here: 1210 us
  waiting for transfers between devices  954 us (78%)
  matrix products  104 us (9%)
  blocking collectives  82.8 us (7%)
  other arithmetic  37.5 us (3%)
  between operations  15.1 us (1%)
    ppermute x5, waiting for transfers between devices, grow_blocks(): other = lax.ppermute(parts, axis, [(i, i ^ apart) for i in range(size)])  396 us
    unnamed x9, waiting for transfers between devices  364 us
    unnamed x2, blocking collectives  82.8 us
    all_gather x1, waiting for transfers between devices, shards(): lax.all_gather(down_weight[layer_idx], ('dp', 'shard'), axis=0, tiled=True)  78.2 us
    all_gather x1, waiting for transfers between devices, shards(): lax.all_gather(up_weight[layer_idx], ('dp', 'shard'), axis=0, tiled=True)  75.5 us
    dot_general x4, matrix products, contract_first(): lax.dot_general(left, right, (((0,), (0,)), ((), ())), preferred_element_...  53.5 us
    all_gather x1, waiting for transfers between devices, shards(): lax.all_gather(attn_weight[layer_idx], ('dp', 'shard'), axis=0, tiled=True)  40.9 us
  transfers between devices with their start and end apart: 11, of which 10 were waited for; matrix products, arithmetic and copies ran while one was open for 8% of the time, Pallas kernels for 0%

profile of v1, /device:TPU:0, one launch (start us, length us, event | category | flops | bytes accessed | tf_op | source)
XLA Modules:
  0.0 1207.4 jit_solution(80014468825780379)
XLA Ops:
  10.4 43.7 %all-reduce = bf16[13056]{0:T(1024)(128)(2,1)S(1)} all-reduce(bf16[13056]{0:T(1024)(128)(2,1)S(1)} %dynamic-update-slice), channel_id=2, replica_groups=mesh['dp'=16,'shard'=2] {'dp','shard'}, use_global_device_ids=true, to_apply=%add | all-reduce | flops 13056 | bytes 52224
  57.4 40.9 %all-gather.8.cloned.1.call-done = bf16[1,4352,1088]{2,1,0:T(8,128)(2,1)} async-done(((bf16[1,136,1088]{2,1,0:T(8,128)(2,1)}), bf16[1,4352,1088]{2,1,0:T(8,128)(2,1)}) %all-gather.8.cloned.1.call-update) | async-done | bytes 9469968 | tf_op jit(solution)/shard_map/all_gather | solution.py:242
  98.4 5.4 fusion.8
  108.3 75.5 %all-gather.10.cloned.1.call-done = bf16[1,4352,1088]{2,1,0:T(8,128)(2,1)} async-done(((bf16[1,136,1088]{2,1,0:T(8,128)(2,1)}), bf16[1,4352,1088]{2,1,0:T(8,128)(2,1)}) %all-gather.10.cloned.1.call-update) | async-done | bytes 9469968 | tf_op jit(solution)/shard_map/all_gather | solution.py:243
  183.9 7.2 fusion.9
  191.1 78.2 %all-gather.12.cloned.1.call-done = bf16[1,4352,1088]{2,1,0:T(8,128)(2,1)} async-done(((bf16[1,136,1088]{2,1,0:T(8,128)(2,1)}), bf16[1,4352,1088]{2,1,0:T(8,128)(2,1)}) %all-gather.12.cloned.1.call-update) | async-done | bytes 9469968 | tf_op jit(solution)/shard_map/all_gather | solution.py:257
  269.4 7.4 fusion.90
  276.8 4.5 multiply_reduce_fusion.1
  293.8 11.0 fusion.26
  304.9 20.0 %convolution_add_fusion = f32[4352,1088]{1,0:T(8,128)} fusion(f32[4352,1088]{1,0:T(8,128)} %fusion.26, bf16[128,1088]{0,1:T(8,128)(2,1)S(1)} %copy-done.26, pred[4352]{0:T(1024)(128)(4,1)S(1)} %iota_compare_fusion.1, bf16[128,1088]{0,1:T(8,128)(2,1)S(1)} %bitcast.106, bf16[128,1088]{0,1:T(8,128)(2,1)S(1)} %bitcast.102, bf16[128,1088]{0,1:T(8,128)(2,1)S(1)} %bitcast.93, ...), kind=kOutput, calls=%fused_computation.1 | convolution fusion | flops 1221902336 | bytes 39276800 | tf_op jit(solution)/shard_map/dot_general | solution.py:54
  324.9 12.6 %fusion.52 = f32[4352,1088]{1,0:T(8,128)} fusion(bf16[128,4352]{1,0:T(8,128)(2,1)} %copy-done.6, f32[128,1088]{0,1:T(8,128)S(1)} %get-tuple-element.35, f32[1088]{0:T(1024)S(1)} %get-tuple-element.16, f32[1088]{0:T(1024)S(1)} %get-tuple-element.15, f32[128]{0:T(128)S(1)} %fusion.74, f32[128]{0:T(128)S(1)} %broadcast_multiply_fusion), kind=kOutput, calls=%fused_computation.90 | convolution fusion | flops 1212850176 | bytes 20620800 | tf_op jit(solution)/shard_map/dot_general | solution.py:54
  338.5 10.0 fusion.82
  351.0 8.1 collective-permute-done
  363.6 34.5 %collective-permute-done.2 = bf16[4,136,1088]{2,1,0:T(8,128)(2,1)S(1)} collective-permute-done((bf16[4,136,1088]{2,1,0:T(8,128)(2,1)S(1)}, bf16[4,136,1088]{2,1,0:T(8,128)(2,1)S(1)}, u32[]{:S(2)}, u32[]{:S(2)}) %collective-permute-start.2) | collective-permute-done | bytes 1183776 | tf_op jit(solution)/shard_map/ppermute | solution.py:21
  400.3 94.7 %collective-permute-done.3 = bf16[8,136,1088]{2,1,0:T(8,128)(2,1)} collective-permute-done((bf16[8,136,1088]{2,1,0:T(8,128)(2,1)S(1)}, bf16[8,136,1088]{2,1,0:T(8,128)(2,1)}, u32[]{:S(2)}, u32[]{:S(2)}) %collective-permute-start.3) | collective-permute-done | bytes 2367520 | tf_op jit(solution)/shard_map/ppermute | solution.py:21
  497.3 3.1 reverse_select_fusion.1
  502.0 256.1 %collective-permute-done.4 = bf16[16,136,1088]{2,1,0:T(8,128)(2,1)} collective-permute-done((bf16[16,136,1088]{2,1,0:T(8,128)(2,1)}, bf16[16,136,1088]{2,1,0:T(8,128)(2,1)}, u32[]{:S(2)}, u32[]{:S(2)}) %collective-permute-start.4) | collective-permute-done | bytes 4735008 | tf_op jit(solution)/shard_map/ppermute | solution.py:21
  758.1 8.9 pad_maximum_fusion
  767.0 14.1 %reverse_select_fusion = bf16[2,16,136,1088]{3,2,1,0:T(8,128)(2,1)} fusion(bf16[2,16,136,1088]{3,2,1,0:T(8,128)(2,1)} %pad_maximum_fusion, pred[]{:T(512)S(6)} %eq.35), kind=kLoop, calls=%fused_computation.2 | loop fusion | flops 4734976 | bytes 18939904 | tf_op jit(solution)/shard_map/jit(_where)/select_n | solution.py:24
  781.3 7.0 fusion.83
  790.1 39.1 %all-reduce.4 = f32[13056]{0:T(1024)S(1)} all-reduce(f32[13056]{0:T(1024)S(1)} %concatenate.13), channel_id=9, replica_groups=mesh['dp'=16,'shard'=2] {'dp','shard'}, use_global_device_ids=true, to_apply=%region_23.24.clone | all-reduce | flops 13056 | bytes 104448
  829.9 8.1 fusion.14
  838.0 142.0 %reduce-scatter.12.cloned.1.call-done = f32[136,1088]{1,0:T(8,128)} async-done(((f32[4352,1088]{1,0:T(8,128)}), f32[136,1088]{1,0:T(8,128)}) %reduce-scatter.12.cloned.1.call-update) | async-done | bytes 591888
  980.0 220.0 %reduce-scatter.14.cloned.1.call-done = f32[136,1088]{1,0:T(8,128)} async-done(((f32[4352,1088]{1,0:T(8,128)}), f32[136,1088]{1,0:T(8,128)}) %reduce-scatter.14.cloned.1.call-update) | async-done | bytes 591888
  (127 shorter events, 40.0 us)
Async XLA Ops:
  7.2 91.2 %all-gather.8.cloned.1.call-start = ((), (), s32[]{:S(2)}) async-start(), calls=%async_computation.3 | async-start | bytes 10340352 | tf_op jit(solution)/shard_map/all_gather | solution.py:242
  7.9 176.0 %all-gather.10.cloned.1.call-start = ((), (), s32[]{:S(2)}) async-start(), calls=%async_computation.4 | async-start | bytes 10340352 | tf_op jit(solution)/shard_map/all_gather | solution.py:243
  8.6 260.7 %all-gather.12.cloned.1.call-start = ((), (), s32[]{:S(2)}) async-start(), calls=%async_computation.5 | async-start | bytes 10340352 | tf_op jit(solution)/shard_map/all_gather | solution.py:257
  9.4 828.7 %reduce-scatter.10.cloned.1.call-start = ((), (), s32[]{:S(2)}) async-start(), calls=%async_computation.6 | async-start | bytes 20680704
  183.9 85.5 %copy-start.17 = (bf16[128,1088]{0,1:T(8,128)(2,1)S(1)}, bf16[128,1088]{0,1:T(8,128)(2,1)}, u32[]{:S(2)}) copy-start(bf16[128,1088]{0,1:T(8,128)(2,1)} %param.13) | copy-start | bytes 835588
  191.1 146.5 %copy-start.1 = (f32[128,4352]{1,0:T(8,128)}, f32[128,4352]{1,0:T(8,128)S(1)}, u32[]{:S(2)}) copy-start(f32[128,4352]{1,0:T(8,128)S(1)} %fusion.9) | copy-start | bytes 6684676
  289.7 15.1 %copy-start.9 = (bf16[17,64,128]{2,1,0:T(8,128)(2,1)}, bf16[17,64,128]{2,1,0:T(8,128)(2,1)S(1)}, u32[]{:S(2)}) copy-start(bf16[17,64,128]{2,1,0:T(8,128)(2,1)S(1)} %get-tuple-element.33) | copy-start | bytes 835588
  293.8 11.0 copy-start.11
  293.8 11.0 copy-start.21
  293.8 11.0 copy-start.24
  293.8 11.0 copy-start.26
  324.9 655.1 %reduce-scatter.12.cloned.1.call-start = ((), (), s32[]{:S(2)}) async-start(), calls=%async_computation.7 | async-start | bytes 20680704
  337.6 862.5 %reduce-scatter.14.cloned.1.call-start = ((), (), s32[]{:S(2)}) async-start(), calls=%async_computation.8 | async-start | bytes 20680704
  349.5 9.6 collective-permute-start
  359.3 2.4 collective-permute-start.1
  362.0 36.1 %collective-permute-start.2 = (bf16[4,136,1088]{2,1,0:T(8,128)(2,1)S(1)}, bf16[4,136,1088]{2,1,0:T(8,128)(2,1)S(1)}, u32[]{:S(2)}, u32[]{:S(2)}) collective-permute-start(bf16[4,136,1088]{2,1,0:T(8,128)(2,1)S(1)} %bitcast.87), channel_id=1, source_target_pairs={{0,4},{1,5},{2,6},{3,7},{4,0},{5,1},{6,2},{7,3},{8,12},{9,13},{10,... | collective-permute-start | bytes 3551240 | tf_op jit(solution)/shard_map/ppermute | solution.py:21
  398.9 96.0 %collective-permute-start.3 = (bf16[8,136,1088]{2,1,0:T(8,128)(2,1)S(1)}, bf16[8,136,1088]{2,1,0:T(8,128)(2,1)}, u32[]{:S(2)}, u32[]{:S(2)}) collective-permute-start(bf16[8,136,1088]{2,1,0:T(8,128)(2,1)S(1)} %bitcast.85), channel_id=1, source_target_pairs={{0,8},{1,9},{2,10},{3,11},{4,12},{5,13},{6,14},{7,15},{8,0},{9,1},... | collective-permute-start | bytes 7102472 | tf_op jit(solution)/shard_map/ppermute | solution.py:21
  500.4 257.8 %collective-permute-start.4 = (bf16[16,136,1088]{2,1,0:T(8,128)(2,1)}, bf16[16,136,1088]{2,1,0:T(8,128)(2,1)}, u32[]{:S(2)}, u32[]{:S(2)}) collective-permute-start(bf16[16,136,1088]{2,1,0:T(8,128)(2,1)} %bitcast.21), channel_id=1, source_target_pairs={{0,16},{1,17},{2,18},{3,19},{4,20},{5,21},{6,22},{7,23},{8,24},{9,... | collective-permute-start | bytes 14204936 | tf_op jit(solution)/shard_map/ppermute | solution.py:21
  767.0 14.2 %copy-start.10 = (bf16[17,64,128]{2,1,0:T(8,128)(2,1)S(1)}, bf16[17,64,128]{2,1,0:T(8,128)(2,1)}, u32[]{:S(2)}) copy-start(bf16[17,64,128]{2,1,0:T(8,128)(2,1)} %copy-done.9) | copy-start | bytes 835588
  767.0 14.2 %copy-start.12 = (bf16[17,64,128]{2,1,0:T(8,128)(2,1)S(1)}, bf16[17,64,128]{2,1,0:T(8,128)(2,1)}, u32[]{:S(2)}) copy-start(bf16[17,64,128]{2,1,0:T(8,128)(2,1)} %convolution_convert_fusion.1) | copy-start | bytes 835588
  767.0 14.2 %copy-start.22 = (bf16[128,17,64]{0,2,1:T(8,128)(2,1)S(1)}, bf16[128,17,64]{0,2,1:T(8,128)(2,1)}, u32[]{:S(2)}) copy-start(bf16[128,17,64]{0,2,1:T(8,128)(2,1)} %get-tuple-element.31) | copy-start | bytes 835588
  781.3 7.5 copy-start.5
  781.3 7.5 copy-start.19
  788.3 41.6 %copy-start.2 = (f32[128,4352]{1,0:T(8,128)S(1)}, f32[128,4352]{1,0:T(8,128)}, u32[]{:S(2)}) copy-start(f32[128,4352]{1,0:T(8,128)} %copy-done.1) | copy-start | bytes 6684676
  (17 other events, 38.3 us)
Sparse Core Ops, SparseCore 0:
  10.8 87.5 all-gather.7
  101.2 82.5 all-gather.9
  186.7 82.5 all-gather.11
  325.0 367.1 reduce-scatter.9
  699.1 280.9 reduce-scatter.11
  986.9 213.1 reduce-scatter.13
